TPU v7x, 32 devices: a whole 2x2x4 slice. The times are simulated.
32 devices in a mesh: batch: 4 (over z), tensor: 8 (over y, x, core).
Axes of the slice: x: 2, y: 2, z: 4, core: 2. Of those that a mesh axis runs over, the one named last changes fastest.
Arguments:
- attn_values: bfloat16 [1024, 8192], P('batch', 'tensor'), may hold values from -6 to 6
- out_weight: bfloat16 [8192, 8192], P('tensor'), may hold values from -0.09375 to 0.09375
- residual_t: bfloat16 [8192, 1024], P('tensor', 'batch'), may hold values from -6 to 6
- projector: bfloat16 [8192, 4096], P('tensor'), may hold values from -0.0625 to 0.0625
- student_input: bfloat16 [1024, 4096], P('batch', 'tensor'), may hold values from -6 to 6
- norm_gain: float32 [4096], replicated, may hold values from 0.1 to 1.9
- w_gate: bfloat16 [4096, 8192], P('batch', 'tensor'), may hold values from -0.09375 to 0.09375
- w_up: bfloat16 [4096, 8192], P('batch', 'tensor'), may hold values from -0.09375 to 0.09375
- w_down: bfloat16 [4096, 8192], P('batch', 'tensor'), may hold values from -0.0625 to 0.0625
- route_index: int32 [4, 64], P('batch'), may hold values from -1 to 255, as said below
Outputs:
- teacher_hidden: bfloat16 [8192, 1024], P('tensor', 'batch')
- grad_gate: float32 [4096, 8192], P('batch', 'tensor')
- grad_up: float32 [4096, 8192], P('batch', 'tensor')
- grad_down: float32 [4096, 8192], P('batch', 'tensor')
Inputs may be any that keep to these rules, and one draw needn't show every extreme that they name: `route_index`: in each batch group the live slots come first, hold distinct positions in increasing order, and the empty slots after them hold -1. The batch groups hold 128 live slots together, and some batch group has all 64 slots live.
All inputs are finite; a program needn't handle non-finite values.
Results may differ from a plain program's by a relative error of at most 0.025.
Values may be sent and summed in bfloat16 or wider, within the bound.
A program may use at most 128 MiB of HBM per device.

v0:
```python
import math

import jax
import jax.numpy as jnp
from jax import lax
from jax.sharding import PartitionSpec as P

epsilon = 1e-05


def grouped_product(left, right):
    dims = (((1,), (1,)), ((0,), (0,)))
    full = lax.dot_general(left, right, dims, preferred_element_type=jnp.float32)
    rounded = lax.optimization_barrier(full.astype(jnp.bfloat16))
    return jnp.sum(rounded.astype(jnp.float32), axis=0)


def on_device(
    attn_values,
    out_weight,
    residual_t,
    projector,
    student_input,
    norm_gain,
    w_gate,
    w_up,
    w_down,
    route_index,
):
    summed = lax.psum_scatter(
        lax.dot_general(
            out_weight, attn_values, (((0,), (1,)), ((), ())), preferred_element_type=jnp.float32
        ).astype(jnp.bfloat16),
        "tensor",
        scatter_dimension=0,
        tiled=True,
    ).astype(jnp.float32)
    teacher_hidden = (residual_t.astype(jnp.float32) + summed).astype(jnp.bfloat16)
    slot_pos = route_index[0]
    present = slot_pos >= 0
    safe_slot = jnp.maximum(slot_pos, 0)
    routed_teacher = jnp.where(present[None, :], jnp.take(teacher_hidden, safe_slot, axis=1), 0)
    target_part = lax.dot_general(
        routed_teacher, projector, (((0,), (0,)), ((), ())), preferred_element_type=jnp.float32
    )
    local_rows = jnp.where(present[:, None], jnp.take(student_input, safe_slot, axis=0), 0)
    routed_input = lax.all_gather(local_rows, "tensor", axis=1, tiled=True).astype(jnp.float32)
    mean_square = jnp.mean(routed_input * routed_input, axis=1, keepdims=True)
    normed = (routed_input * lax.rsqrt(mean_square + epsilon) * norm_gain[None, :]).astype(
        jnp.bfloat16
    )
    slot_total = normed.shape[0]
    local_units = w_gate.shape[1]
    gate_full, up_full, down_full = (
        lax.all_gather(w_gate, "batch", axis=0, tiled=True),
        lax.all_gather(w_up, "batch", axis=0, tiled=True),
        lax.all_gather(w_down, "batch", axis=0, tiled=True),
    )
    gate_act = jnp.dot(normed, gate_full, preferred_element_type=jnp.float32)
    up_act = jnp.dot(normed, up_full, preferred_element_type=jnp.float32)
    sigma_gate = jax.nn.sigmoid(gate_act)
    hidden = (gate_act * sigma_gate * up_act).astype(jnp.bfloat16)
    out_part = lax.dot_general(
        hidden, down_full, (((1,), (1,)), ((), ())), preferred_element_type=jnp.float32
    )
    student_out, target = (
        lax.psum(out_part.astype(jnp.bfloat16), "tensor").astype(jnp.float32),
        lax.psum(target_part.astype(jnp.bfloat16), "tensor").astype(jnp.float32),
    )
    misfit = student_out - target
    group_count = lax.axis_size("batch")
    mean_routed = student_input.shape[0] // 8
    loss_scale = 1.0 / math.sqrt(mean_routed * group_count)
    grad_out = (jnp.where(present[:, None], misfit, 0.0) * loss_scale).astype(jnp.bfloat16)
    grad_hidden = jnp.dot(grad_out, down_full, preferred_element_type=jnp.float32)
    grad_gate_act = (
        grad_hidden * up_act * sigma_gate * (1.0 + gate_act * (1.0 - sigma_gate))
    ).astype(jnp.bfloat16)
    grad_up_act = (grad_hidden * gate_act * sigma_gate).astype(jnp.bfloat16)
    rows_local = w_gate.shape[0]
    every_normed, every_grad = (
        lax.all_to_all(normed, "batch", split_axis=1, concat_axis=0, tiled=True),
        lax.all_to_all(grad_out, "batch", split_axis=1, concat_axis=0, tiled=True),
    )
    every_gate, every_up, every_hidden = (
        lax.all_gather(grad_gate_act, "batch", axis=0, tiled=True),
        lax.all_gather(grad_up_act, "batch", axis=0, tiled=True),
        lax.all_gather(hidden, "batch", axis=0, tiled=True),
    )
    normed_groups = every_normed.reshape(group_count, slot_total, rows_local)
    grad_groups = every_grad.reshape(group_count, slot_total, rows_local)
    gate_groups = every_gate.reshape(group_count, slot_total, local_units)
    up_groups = every_up.reshape(group_count, slot_total, local_units)
    hidden_groups = every_hidden.reshape(group_count, slot_total, local_units)
    grad_gate = grouped_product(normed_groups, gate_groups)
    grad_up = grouped_product(normed_groups, up_groups)
    grad_down = grouped_product(grad_groups, hidden_groups)
    return (teacher_hidden, grad_gate, grad_up, grad_down)


def solution(mesh):
    in_specs = (
        P("batch", "tensor"),
        P("tensor", None),
        P("tensor", "batch"),
        P("tensor", None),
        P("batch", "tensor"),
        P(),
        P("batch", "tensor"),
        P("batch", "tensor"),
        P("batch", "tensor"),
        P("batch", None),
    )
    out_specs = (
        P("tensor", "batch"),
        P("batch", "tensor"),
        P("batch", "tensor"),
        P("batch", "tensor"),
    )
    return jax.shard_map(
        on_device, mesh=mesh, in_specs=in_specs, out_specs=out_specs, check_vma=False
    )
```

profile of v0, /device:TPU:0, one launch (start us, length us, event | category | flops | bytes accessed | tf_op | source)
XLA Modules:
  0.0 617.1 jit_solution(13908110257670186646)
XLA Ops:
  8.0 0.0 copy-start
  8.0 0.0 reduce-scatter.2.cloned.1.call-start
  8.1 1.0 copy-done
  9.0 12.6 %convolution_convert_fusion = bf16[8192,256]{1,0:T(8,128)(2,1)} fusion(bf16[1024,8192]{1,0:T(8,128)(2,1)} %param.11, bf16[256,1024]{1,0:T(8,128)(2,1)S(1)} %copy-done), kind=kOutput, calls=%fused_computation.5 | convolution fusion | flops 4297064448 | bytes 21495808 | tf_op jit(solution)/shard_map/dot_general | solution.py:31
  21.7 0.0 reduce-scatter.2.cloned.1.call-update
  21.7 0.0 all-gather.4.cloned.1.call-start
  21.7 0.5 all-gather.4.cloned.1.call-update
  22.3 0.0 all-gather.6.cloned.1.call-start
  22.3 0.5 all-gather.6.cloned.1.call-update
  22.8 0.0 all-gather.8.cloned.1.call-start
  22.9 0.5 all-gather.8.cloned.1.call-update
  23.4 0.0 all-reduce.3.cloned.1.call-start
  23.5 0.7 gather_fusion
  24.2 0.1 select_select_fusion
  24.3 11.5 %all_gather.21 = bf16[64,4096]{1,0:T(8,128)(2,1)S(1)} all-gather(bf16[64,512]{1,0:T(8,128)(2,1)S(1)} %select_select_fusion), channel_id=1, replica_groups=mesh['batch'=4,'tensor'=8] {'tensor'}, dimensions={1}, use_global_device_ids=true | all-gather | bytes 589824 | tf_op jit(solution)/shard_map/all_gather | solution.py:47
  35.9 0.2 fusion
  36.1 0.2 fusion.2
  36.3 39.5 %reduce-scatter.2.cloned.1.call-done = bf16[1024,256]{1,0:T(8,128)(2,1)} async-done(((bf16[8192,256]{1,0:T(8,128)(2,1)}), bf16[1024,256]{1,0:T(8,128)(2,1)}) %reduce-scatter.2.cloned.1.call-update) | async-done | bytes 524304 | tf_op jit(solution)/shard_map/reduce_scatter | solution.py:30
  75.7 0.0 copy-done.4
  75.7 1.2 add_convert_fusion
  76.9 0.0 copy-start.2
  76.9 0.2 copy.17
  77.2 0.7 gather_fusion.1
  77.9 5.9 convolution_convert_fusion.4
  83.7 92.2 %all-gather.4.cloned.1.call-done = bf16[4096,1024]{1,0:T(8,128)(2,1)} async-done(((bf16[1024,1024]{1,0:T(8,128)(2,1)}), bf16[4096,1024]{1,0:T(8,128)(2,1)}) %all-gather.4.cloned.1.call-update) | async-done | bytes 8388624 | tf_op jit(solution)/shard_map/all_gather | solution.py:55
  176.0 4.9 fusion.14
  180.9 144.2 %all-gather.6.cloned.1.call-done = bf16[4096,1024]{1,0:T(8,128)(2,1)} async-done(((bf16[1024,1024]{1,0:T(8,128)(2,1)}), bf16[4096,1024]{1,0:T(8,128)(2,1)}) %all-gather.6.cloned.1.call-update) | async-done | bytes 8388624 | tf_op jit(solution)/shard_map/all_gather | solution.py:56
  325.1 5.0 multiply_convert_fusion.3
  330.1 144.2 %all-gather.8.cloned.1.call-done = bf16[4096,1024]{1,0:T(8,128)(2,1)} async-done(((bf16[1024,1024]{1,0:T(8,128)(2,1)}), bf16[4096,1024]{1,0:T(8,128)(2,1)}) %all-gather.8.cloned.1.call-update) | async-done | bytes 8388624 | tf_op jit(solution)/shard_map/all_gather | solution.py:57
  474.2 6.8 %convolution_convert_fusion.5 = bf16[64,4096]{1,0:T(8,128)(2,1)} fusion(bf16[64,1024]{1,0:T(8,128)(2,1)S(1)} %get-tuple-element.10, bf16[4096,1024]{1,0:T(8,128)(2,1)} %all-gather.8.cloned.1.call-done), kind=kOutput, calls=%fused_computation.10 | convolution fusion | flops 537133056 | bytes 9043968 | tf_op jit(solution)/shard_map/dot_general | solution.py:63
  481.1 0.0 all-reduce.3.cloned.1.call-update
  481.1 0.8 copy.24
  481.9 3.5 all-to-all-start
  485.4 24.8 %all_gather.27 = bf16[256,1024]{1,0:T(8,128)(2,1)S(1)} all-gather(bf16[64,1024]{1,0:T(8,128)(2,1)S(1)} %get-tuple-element.10), channel_id=1, replica_groups=mesh['batch'=4,'tensor'=8] {'batch'}, dimensions={0}, use_global_device_ids=true | all-gather | bytes 655360 | tf_op jit(solution)/shard_map/all_gather | solution.py:88
  510.2 26.0 %all-reduce.3.cloned.1.call-done = (bf16[64,4096]{1,0:T(8,128)(2,1)}, bf16[64,4096]{1,0:T(8,128)(2,1)}) async-done(((bf16[64,4096]{1,0:T(8,128)(2,1)}, bf16[64,4096]{1,0:T(8,128)(2,1)}), (bf16[64,4096]{1,0:T(8,128)(2,1)}, bf16[64,4096]{1,0:T(8,128)(2,1)})) %all-reduce.3.cloned.1.call-update) | async-done | bytes 1048592 | tf_op jit(solution)/shard_map/psum | solution.py:68
  536.2 1.4 multiply_convert_fusion
  537.6 5.0 multiply_convert_fusion.1
  542.6 14.9 %all_gather.25 = bf16[256,1024]{1,0:T(8,128)(2,1)S(1)} all-gather(bf16[64,1024]{1,0:T(8,128)(2,1)S(1)} %get-tuple-element.7), channel_id=1, replica_groups=mesh['batch'=4,'tensor'=8] {'batch'}, dimensions={0}, use_global_device_ids=true | all-gather | bytes 655360 | tf_op jit(solution)/shard_map/all_gather | solution.py:86
  557.5 0.0 all-to-all-done
  557.5 5.6 convolution_convert_fusion.3
  563.1 16.4 %all_gather.26 = bf16[256,1024]{1,0:T(8,128)(2,1)S(1)} all-gather(bf16[64,1024]{1,0:T(8,128)(2,1)S(1)} %get-tuple-element.6), channel_id=1, replica_groups=mesh['batch'=4,'tensor'=8] {'batch'}, dimensions={0}, use_global_device_ids=true | all-gather | bytes 655360 | tf_op jit(solution)/shard_map/all_gather | solution.py:87
  579.5 5.6 convolution_convert_fusion.2
  585.1 0.8 copy.23
  585.9 5.2 all-to-all-start.1
  591.2 11.9 %convert_reduce_fusion.1 = (f32[1024,1024]{1,0:T(8,128)}, f32[1024,1024]{1,0:T(8,128)}) fusion(bf16[4,1024,1024]{2,1,0:T(8,128)(2,1)} %convolution_convert_fusion.2, bf16[4,1024,1024]{2,1,0:T(8,128)(2,1)} %convolution_convert_fusion.3), kind=kLoop, calls=%fused_computation.3 | loop fusion | flops 14680064 | bytes 25165824 | tf_op jit(solution)/shard_map/reduce_sum | solution.py:15
  603.0 0.0 all-to-all-done.1
  603.0 2.4 convolution_convert_fusion.1
  605.4 4.1 convert_reduce_fusion
  (14 shorter events, 0.0 us)
Async XLA Ops:
  8.0 1.1 copy-start
  8.0 67.7 %reduce-scatter.2.cloned.1.call-start = ((), (), s32[]{:S(2)}) async-start(), calls=%async_computation.3 | async-start | bytes 4718592 | tf_op jit(solution)/shard_map/reduce_scatter | solution.py:30
  21.6 1.8 copy-start.6
  21.6 1.9 copy-start.3
  21.6 14.4 %copy-start.5 = (f32[4096]{0:T(1024)S(1)}, f32[4096]{0:T(1024)}, u32[]{:S(2)}) copy-start(f32[4096]{0:T(1024)} %param.15) | copy-start | bytes 49156
  21.6 54.1 %copy-start.4 = (bf16[1024,256]{1,0:T(8,128)(2,1)S(1)}, bf16[1024,256]{1,0:T(8,128)(2,1)}, u32[]{:S(2)}) copy-start(bf16[1024,256]{1,0:T(8,128)(2,1)} %param.12) | copy-start | bytes 1572868
  21.7 154.3 %all-gather.4.cloned.1.call-start = ((), (), s32[]{:S(2)}) async-start(), calls=%async_computation.4 | async-start | bytes 10485760 | tf_op jit(solution)/shard_map/all_gather | solution.py:55
  22.3 302.8 %all-gather.6.cloned.1.call-start = ((), (), s32[]{:S(2)}) async-start(), calls=%async_computation.5 | async-start | bytes 10485760 | tf_op jit(solution)/shard_map/all_gather | solution.py:56
  22.8 451.4 %all-gather.8.cloned.1.call-start = ((), (), s32[]{:S(2)}) async-start(), calls=%async_computation.6 | async-start | bytes 10485760 | tf_op jit(solution)/shard_map/all_gather | solution.py:57
  23.4 512.8 %all-reduce.3.cloned.1.call-start = ((), (), s32[]{:S(2)}) async-start(), calls=%async_computation.7 | async-start | bytes 2097152 | tf_op jit(solution)/shard_map/psum | solution.py:68
  76.9 6.8 %copy-start.2 = (bf16[1024,256]{1,0:T(8,128)(2,1)}, bf16[1024,256]{1,0:T(8,128)(2,1)S(1)}, u32[]{:S(2)}) copy-start(bf16[1024,256]{1,0:T(8,128)(2,1)S(1)} %add_convert_fusion) | copy-start | bytes 1572868
  481.9 75.6 %all-to-all-start = ((bf16[64,4,1024]{2,0,1:T(8,128)(2,1)}), bf16[64,4,1024]{2,0,1:T(8,128)(2,1)S(1)}, u32[]{:S(2)}, u32[]{:S(2)}) async-start(bf16[64,4,1024]{2,0,1:T(8,128)(2,1)} %bitcast.38), calls=%async_computation.1 | async-start | bytes 1048576 | tf_op jit(solution)/shard_map/all_to_all | solution.py:82
  585.9 17.1 %all-to-all-start.1 = ((bf16[64,4,1024]{2,0,1:T(8,128)(2,1)}), bf16[64,4,1024]{2,0,1:T(8,128)(2,1)S(1)}, u32[]{:S(2)}, u32[]{:S(2)}) async-start(bf16[64,4,1024]{2,0,1:T(8,128)(2,1)} %bitcast.37), calls=%async_computation.2 | async-start | bytes 1048576 | tf_op jit(solution)/shard_map/all_to_all | solution.py:83
  603.0 6.5 %copy-start.1 = (bf16[256,1024]{1,0:T(8,128)(2,1)S(1)}, bf16[256,1024]{1,0:T(8,128)(2,1)}, u32[]{:S(2)}) copy-start(bf16[256,1024]{1,0:T(8,128)(2,1)} %param.10) | copy-start | bytes 1572868
Sparse Core Ops, SparseCore 0:
  21.8 53.8 reduce-scatter.1
  481.2 54.9 all-reduce.2
Sparse Core Ops, SparseCore 1:
  23.7 152.2 all-gather.3
  177.4 147.6 all-gather.5
  326.5 147.6 all-gather.7
where the time goes:
time: 618 us; the launch traced here: 617 us
  waiting for transfers between devices  448 us (72%)
  blocking collectives  67.6 us (11%)
  matrix products  53.8 us (9%)
  other arithmetic  19.1 us (3%)
  between operations  15.8 us (3%)
  starting transfers between devices  8.92 us (1%)
    all_gather x1, waiting for transfers between devices, on_device(): lax.all_gather(w_up, 'batch', axis=0, tiled=True)  144 us
    all_gather x1, waiting for transfers between devices, on_device(): lax.all_gather(w_down, 'batch', axis=0, tiled=True)  144 us
    all_gather x1, waiting for transfers between devices, on_device(): lax.all_gather(w_gate, 'batch', axis=0, tiled=True)  92.2 us
    reduce_scatter x1, waiting for transfers between devices, on_device(): lax.psum_scatter(lax.dot_general(out_weight, attn_values, (((0,), (1,)),...  39.5 us
    psum x1, waiting for transfers between devices, on_device(): lax.psum(target_part.astype(jnp.bfloat16), 'tensor').astype(jnp.float32)  26 us
    all_gather x1, blocking collectives, on_device(): lax.all_gather(hidden, 'batch', axis=0, tiled=True)  24.8 us
    all_gather x1, blocking collectives, on_device(): lax.all_gather(grad_up_act, 'batch', axis=0, tiled=True)  16.4 us
    reduce_sum x2, other arithmetic, grouped_product(): return jnp.sum(rounded.astype(jnp.float32), axis=0)  16 us
  transfers between devices with their start and end apart: 7, of which 5 were waited for; matrix products, arithmetic and copies ran while one was open for 6% of the time, Pallas kernels for 0%

commit v1 on v0

v1 whole, which is shorter than its diff:
```python
import math

import jax
import jax.numpy as jnp
from jax import lax
from jax.sharding import PartitionSpec as P

epsilon = 1e-05
f32 = jnp.float32
bf16 = jnp.bfloat16


def contract(left, right, left_dim, right_dim):
    return lax.dot_general(
        left, right, (((left_dim,), (right_dim,)), ((), ())), preferred_element_type=f32
    )


def on_device(
    attn_values,
    out_weight,
    residual_t,
    projector,
    student_input,
    norm_gain,
    w_gate,
    w_up,
    w_down,
    route_index,
):
    group_count = lax.axis_size("batch")
    mean_routed = student_input.shape[0] // 8
    routed = mean_routed * group_count
    loss_scale = 1.0 / math.sqrt(routed)

    every_route = lax.all_gather(route_index, "batch", axis=0, tiled=True).reshape(-1)
    live = every_route >= 0
    rank = jnp.cumsum(live.astype(jnp.int32)) - 1
    row_ids = lax.broadcasted_iota(jnp.int32, (routed, live.shape[0]), 0)
    select = ((rank[None, :] == row_ids) & live[None, :]).astype(bf16)
    live_row = lax.broadcasted_iota(jnp.int32, (routed, 1), 0) <= rank[-1]

    slot_pos = route_index[0]
    present = slot_pos >= 0
    safe_slot = jnp.maximum(slot_pos, 0)
    local_rows = jnp.where(present[:, None], jnp.take(student_input, safe_slot, axis=0), 0)
    routed_input = lax.all_gather(local_rows, "tensor", axis=1, tiled=True).astype(f32)
    mean_square = jnp.mean(routed_input * routed_input, axis=1, keepdims=True)
    normed = (routed_input * lax.rsqrt(mean_square + epsilon) * norm_gain[None, :]).astype(bf16)
    every_normed = lax.all_to_all(normed, "batch", split_axis=1, concat_axis=0, tiled=True)

    summed = lax.psum_scatter(
        contract(out_weight, attn_values, 0, 1).astype(bf16),
        "tensor",
        scatter_dimension=0,
        tiled=True,
    ).astype(f32)
    teacher_hidden = (residual_t.astype(f32) + summed).astype(bf16)

    rows = contract(select, every_normed, 1, 0).astype(bf16)
    gate_up = lax.psum(
        jnp.stack([contract(rows, w_gate, 1, 0), contract(rows, w_up, 1, 0)]).astype(bf16),
        "batch",
    ).astype(f32)
    gate_act, up_act = gate_up[0], gate_up[1]
    sigma_gate = jax.nn.sigmoid(gate_act)
    hidden = (gate_act * sigma_gate * up_act).astype(bf16)
    out_part = contract(hidden, w_down, 1, 1)

    routed_teacher = jnp.where(present[None, :], jnp.take(teacher_hidden, safe_slot, axis=1), 0)
    target_part = contract(routed_teacher, projector, 0, 0).astype(bf16)
    every_target = lax.all_to_all(target_part, "batch", split_axis=1, concat_axis=0, tiled=True)
    target_rows = contract(select, every_target, 1, 0)

    misfit = lax.psum((out_part - target_rows).astype(bf16), "tensor").astype(f32)
    grad_out = (jnp.where(live_row, misfit, 0.0) * loss_scale).astype(bf16)
    grad_hidden = lax.psum(contract(grad_out, w_down, 1, 0).astype(bf16), "batch").astype(f32)
    grad_gate_act = (
        grad_hidden * up_act * sigma_gate * (1.0 + gate_act * (1.0 - sigma_gate))
    ).astype(bf16)
    grad_up_act = (grad_hidden * gate_act * sigma_gate).astype(bf16)
    grad_gate = contract(rows, grad_gate_act, 0, 0)
    grad_up = contract(rows, grad_up_act, 0, 0)
    grad_down = contract(grad_out, hidden, 0, 0)
    return (teacher_hidden, grad_gate, grad_up, grad_down)


def solution(mesh):
    in_specs = (
        P("batch", "tensor"),
        P("tensor", None),
        P("tensor", "batch"),
        P("tensor", None),
        P("batch", "tensor"),
        P(),
        P("batch", "tensor"),
        P("batch", "tensor"),
        P("batch", "tensor"),
        P("batch", None),
    )
    out_specs = (
        P("tensor", "batch"),
        P("batch", "tensor"),
        P("batch", "tensor"),
        P("batch", "tensor"),
    )
    return jax.shard_map(
        on_device, mesh=mesh, in_specs=in_specs, out_specs=out_specs, check_vma=False
    )
```

time: 618 us -> 220 us (0.36)
  waiting for transfers between devices: 448 us -> 118 us
  blocking collectives: 67.6 us -> 26.4 us
  matrix products: 53.8 us -> 38.5 us
  other arithmetic: 19.1 us -> 5.09 us
    all_gather x3 -> x0, waiting for transfers between devices: 381 us -> none  [the longest x1 144 us: on_device(): lax.all_gather(w_up, 'batch', axis=0, tiled=True)]
    psum x1 -> x3, waiting for transfers between devices: 26 us -> 104 us  [the longest x1 51.9 us: on_device(): lax.psum((out_part - target_rows).astype(bf16), 'tensor').astype(f32)]
    all_gather x4 -> x2, blocking collectives: 67.6 us -> 26.4 us  [the longest x1 15.1 us: on_device(): lax.all_gather(route_index, 'batch', axis=0, tiled=True).reshape(-1)]
    reduce_scatter x1, waiting for transfers between devices: 39.5 us -> 13.7 us  [on_device(): lax.psum_scatter(contract(out_weight, attn_values, 0, 1).astype(bf16), 't...]
    reduce_sum x2 -> x0, other arithmetic: 16 us -> none  [grouped_product(): return jnp.sum(rounded.astype(jnp.float32), axis=0)]
    dot_general x9 -> x11, matrix products: 53.8 us -> 38.5 us  [contract(): lax.dot_general(left, right, (((left_dim,), (right_dim,)), ((), ())), pre...]
  transfers between devices with their start and end apart: 7 -> 6, of which waited for: 5 -> 4; matrix products, arithmetic and copies ran while one was open for 6% -> 11% of each run, Pallas kernels for 0% -> 0%
where the time goes in v1:
time: 220 us; the launch traced here: 219 us
  waiting for transfers between devices  118 us (54%)
  matrix products  38.5 us (18%)
  blocking collectives  26.4 us (12%)
  between operations  15.6 us (7%)
  starting transfers between devices  9.72 us (4%)
  local copies, waits for them, and re-layouts  5.87 us (3%)
  other arithmetic  5.09 us (2%)
    psum x1, waiting for transfers between devices, on_device(): lax.psum((out_part - target_rows).astype(bf16), 'tensor').astype(f32)  51.9 us
    dot_general x11, matrix products, contract(): lax.dot_general(left, right, (((left_dim,), (right_dim,)), ((), ())), pre...  38.5 us
    psum x1, waiting for transfers between devices, on_device(): lax.psum(contract(grad_out, w_down, 1, 0).astype(bf16), 'batch').astype(f32)  31.2 us
    psum x1, waiting for transfers between devices, on_device(): lax.psum(jnp.stack([contract(rows, w_gate, 1, 0), contract(rows, w_up, 1,...  20.9 us
    all_gather x1, blocking collectives, on_device(): lax.all_gather(route_index, 'batch', axis=0, tiled=True).reshape(-1)  15.1 us
    reduce_scatter x1, waiting for transfers between devices, on_device(): lax.psum_scatter(contract(out_weight, attn_values, 0, 1).astype(bf16), 't...  13.7 us
    all_gather x1, blocking collectives, on_device(): lax.all_gather(local_rows, 'tensor', axis=1, tiled=True).astype(f32)  11.3 us
    all_to_all x1, starting transfers between devices, on_device(): lax.all_to_all(normed, 'batch', split_axis=1, concat_axis=0, tiled=True)  4.88 us
  transfers between devices with their start and end apart: 6, of which 4 were waited for; matrix products, arithmetic and copies ran while one was open for 11% of the time, Pallas kernels for 0%

profile of v1, /device:TPU:0, one launch (start us, length us, event | category | flops | bytes accessed | tf_op | source)
XLA Modules:
  0.0 219.0 jit_solution(1372493965214231612)
XLA Ops:
  8.0 0.0 reduce-scatter.2.cloned.1.call-start
  8.1 12.8 %convolution_convert_fusion = bf16[8192,256]{1,0:T(8,128)(2,1)} fusion(bf16[1024,8192]{1,0:T(8,128)(2,1)} %param.11, bf16[256,1024]{1,0:T(8,128)(2,1)} %param.10), kind=kOutput, calls=%fused_computation.2 | convolution fusion | flops 4297064448 | bytes 21495808 | tf_op jit(solution)/shard_map/dot_general | solution.py:14
  20.8 0.0 reduce-scatter.2.cloned.1.call-update
  20.9 0.6 copy-done.8
  21.5 0.3 copy-done.4
  21.8 0.7 gather_fusion
  22.5 0.1 select_select_fusion
  22.6 11.3 %all_gather.7 = bf16[64,4096]{1,0:T(8,128)(2,1)S(1)} all-gather(bf16[64,512]{1,0:T(8,128)(2,1)S(1)} %select_select_fusion), channel_id=1, replica_groups=mesh['batch'=4,'tensor'=8] {'tensor'}, dimensions={1}, use_global_device_ids=true | all-gather | bytes 589824 | tf_op jit(solution)/shard_map/all_gather | solution.py:47
  33.9 0.2 fusion.3
  34.2 0.2 fusion.5
  34.4 0.8 copy.26
  35.2 4.9 %all-to-all-start = ((bf16[64,4,1024]{2,0,1:T(8,128)(2,1)}), bf16[64,4,1024]{2,0,1:T(8,128)(2,1)S(1)}, u32[]{:S(2)}, u32[]{:S(2)}) async-start(bf16[64,4,1024]{2,0,1:T(8,128)(2,1)} %bitcast.59), calls=%async_computation.1 | async-start | bytes 1048576 | tf_op jit(solution)/shard_map/all_to_all | solution.py:50
  40.1 15.1 %all-gather = s32[4,1,64]{2,1,0:T(1,128)S(1)} all-gather(s32[1,1,64]{2,1,0:T(1,128)S(1)} %bitcast.63), channel_id=1, replica_groups=mesh['batch'=4,'tensor'=8] {'batch'}, dimensions={0}, use_global_device_ids=true | all-gather | bytes 1280 | tf_op jit(solution)/shard_map/all_gather | solution.py:36
  55.2 0.1 reshape.96
  55.2 0.3 reduce-window.9
  55.6 0.1 slice.16
  55.7 0.1 ge.39
  55.8 0.1 slice_reduce_fusion
  55.9 0.1 add_bitcast_fusion
  56.0 0.2 convolution_convert_fusion.5
  56.2 2.0 fusion.2
  58.3 2.0 fusion.1
  60.3 0.8 pad_maximum_fusion
  61.2 0.0 all-reduce.4.cloned.1.call-update
  61.2 13.7 %reduce-scatter.2.cloned.1.call-done = bf16[1024,256]{1,0:T(8,128)(2,1)} async-done(((bf16[8192,256]{1,0:T(8,128)(2,1)}), bf16[1024,256]{1,0:T(8,128)(2,1)}) %reduce-scatter.2.cloned.1.call-update) | async-done | bytes 524304 | tf_op jit(solution)/shard_map/reduce_scatter | solution.py:52
  74.9 1.3 add_convert_fusion
  76.2 0.2 copy.19
  76.5 0.7 gather_fusion.1
  77.2 5.1 %convolution_convert_fusion.1 = bf16[64,4096]{1,0:T(8,128)(2,1)S(1)} fusion(bf16[1024,4096]{1,0:T(8,128)(2,1)} %param.13, bf16[64,1024]{1,0:T(8,128)(2,1)S(1)} %gather_fusion.1, pred[64]{0:T(512)(128)(4,1)S(1)} %get-tuple-element.4, pred[64]{0:T(512)(128)(4,1)S(1)} %get-tuple-element.5), kind=kOutput, calls=%fused_computation.3 | convolution fusion | flops 537264128 | bytes 9044096 | tf_op jit(solution)/shard_map/dot_general | solution.py:14
  82.3 0.8 copy.25
  83.1 4.6 %all-to-all-start.1 = ((bf16[64,4,1024]{2,0,1:T(8,128)(2,1)}), bf16[64,4,1024]{2,0,1:T(8,128)(2,1)}, u32[]{:S(2)}, u32[]{:S(2)}) async-start(bf16[64,4,1024]{2,0,1:T(8,128)(2,1)} %bitcast.58), calls=%async_computation.2 | async-start | bytes 1048576 | tf_op jit(solution)/shard_map/all_to_all | solution.py:72
  87.7 20.9 %all-reduce.4.cloned.1.call-done = bf16[2,128,1024]{2,1,0:T(8,128)(2,1)} async-done(((bf16[2,128,1024]{2,1,0:T(8,128)(2,1)}), bf16[2,128,1024]{2,1,0:T(8,128)(2,1)}) %all-reduce.4.cloned.1.call-update) | async-done | bytes 524304 | tf_op jit(solution)/shard_map/psum | solution.py:61
  108.6 1.1 convert_element_type.73
  109.7 0.2 multiply_convert_fusion.1
  109.9 0.7 copy-done.1
  110.6 1.6 fusion.40
  112.2 2.1 fusion
  114.3 0.0 all-reduce.6.cloned.1.call-update
  114.4 0.2 all-reduce.8.cloned.1.call-start
  114.6 0.6 slice.18
  115.2 0.6 iota_compare_fusion.1
  115.8 51.9 %all-reduce.6.cloned.1.call-done = bf16[128,1024]{1,0:T(8,128)(2,1)} async-done(((bf16[128,1024]{1,0:T(8,128)(2,1)}), bf16[128,1024]{1,0:T(8,128)(2,1)}) %all-reduce.6.cloned.1.call-update) | async-done | bytes 262160 | tf_op jit(solution)/shard_map/psum | solution.py:75
  167.7 2.1 convolution_convert_fusion.2
  169.9 0.0 all-reduce.8.cloned.1.call-update
  169.9 3.9 %fusion.24 = f32[1024,1024]{1,0:T(8,128)} fusion(bf16[128,1024]{1,0:T(8,128)(2,1)} %copy-done.1, bf16[128,1024]{1,0:T(8,128)(2,1)} %all-reduce.6.cloned.1.call-done, pred[128]{0:T(512)(128)(4,1)S(1)} %iota_compare_fusion.1), kind=kOutput, calls=%fused_computation.43 | convolution fusion | flops 268959744 | bytes 4718720 | tf_op jit(solution)/shard_map/dot_general | solution.py:14
  173.8 31.2 %all-reduce.8.cloned.1.call-done = bf16[128,1024]{1,0:T(8,128)(2,1)} async-done(((bf16[128,1024]{1,0:T(8,128)(2,1)}), bf16[128,1024]{1,0:T(8,128)(2,1)}) %all-reduce.8.cloned.1.call-update) | async-done | bytes 262160 | tf_op jit(solution)/shard_map/psum | solution.py:77
  205.0 3.8 %fusion.13 = f32[1024,1024]{1,0:T(8,128)} fusion(bf16[128,1024]{1,0:T(8,128)(2,1)S(1)} %convolution_convert_fusion.5, bf16[128,1024]{1,0:T(8,128)(2,1)} %all-reduce.8.cloned.1.call-done, f32[2,128,1024]{2,1,0:T(8,128)S(1)} %convert_element_type.73), kind=kOutput, calls=%fused_computation.34 | convolution fusion | flops 269877248 | bytes 5767168 | tf_op jit(solution)/shard_map/dot_general | solution.py:14
  208.8 2.8 %fusion.11 = f32[1024,1024]{1,0:T(8,128)} fusion(bf16[128,1024]{1,0:T(8,128)(2,1)S(1)} %convolution_convert_fusion.5, bf16[128,1024]{1,0:T(8,128)(2,1)S(1)} %copy-done.3, f32[2,128,1024]{2,1,0:T(8,128)S(1)} %convert_element_type.73), kind=kOutput, calls=%fused_computation.33 | convolution fusion | flops 269352960 | bytes 5242880 | tf_op jit(solution)/shard_map/dot_general | solution.py:14
  (26 shorter events, 0.2 us)
Async XLA Ops:
  8.0 102.6 %copy-start = (bf16[1024,1024]{1,0:T(8,128)(2,1)S(1)}, bf16[1024,1024]{1,0:T(8,128)(2,1)}, u32[]{:S(2)}) copy-start(bf16[1024,1024]{1,0:T(8,128)(2,1)} %param.18) | copy-start | bytes 6291460
  8.0 66.9 %reduce-scatter.2.cloned.1.call-start = ((), (), s32[]{:S(2)}) async-start(), calls=%async_computation.3 | async-start | bytes 4718592 | tf_op jit(solution)/shard_map/reduce_scatter | solution.py:52
  20.8 0.7 copy-start.8
  20.8 1.0 copy-start.4
  20.8 13.3 %copy-start.5 = (f32[4096]{0:T(1024)S(1)}, f32[4096]{0:T(1024)}, u32[]{:S(2)}) copy-start(f32[4096]{0:T(1024)} %param.15) | copy-start | bytes 49156
  35.2 20.8 %all-to-all-start = ((bf16[64,4,1024]{2,0,1:T(8,128)(2,1)}), bf16[64,4,1024]{2,0,1:T(8,128)(2,1)S(1)}, u32[]{:S(2)}, u32[]{:S(2)}) async-start(bf16[64,4,1024]{2,0,1:T(8,128)(2,1)} %bitcast.59), calls=%async_computation.1 | async-start | bytes 1048576 | tf_op jit(solution)/shard_map/all_to_all | solution.py:50
  40.1 68.5 %all-reduce.4.cloned.1.call-start = ((), (), s32[]{:S(2)}) async-start(), calls=%async_computation.4 | async-start | bytes 1048576 | tf_op jit(solution)/shard_map/psum | solution.py:61
  55.8 5.4 %copy-start.6 = (pred[256]{0:T(512)(128)(4,1)}, pred[256]{0:T(512)(128)(4,1)S(1)}, u32[]{:S(2)}) copy-start(pred[256]{0:T(512)(128)(4,1)S(1)} %ge.39) | copy-start | bytes 772
  76.2 6.0 %copy-start.2 = (bf16[1024,256]{1,0:T(8,128)(2,1)}, bf16[1024,256]{1,0:T(8,128)(2,1)S(1)}, u32[]{:S(2)}) copy-start(bf16[1024,256]{1,0:T(8,128)(2,1)S(1)} %add_convert_fusion) | copy-start | bytes 1572868
  82.3 29.9 %copy-start.7 = (pred[256]{0:T(512)(128)(4,1)S(1)}, pred[256]{0:T(512)(128)(4,1)}, u32[]{:S(2)}) copy-start(pred[256]{0:T(512)(128)(4,1)} %copy-done.6) | copy-start | bytes 772
  83.1 29.1 %all-to-all-start.1 = ((bf16[64,4,1024]{2,0,1:T(8,128)(2,1)}), bf16[64,4,1024]{2,0,1:T(8,128)(2,1)}, u32[]{:S(2)}, u32[]{:S(2)}) async-start(bf16[64,4,1024]{2,0,1:T(8,128)(2,1)} %bitcast.58), calls=%async_computation.2 | async-start | bytes 1048576 | tf_op jit(solution)/shard_map/all_to_all | solution.py:72
  87.7 80.1 %all-reduce.6.cloned.1.call-start = ((), (), s32[]{:S(2)}) async-start(), calls=%async_computation.5 | async-start | bytes 524288 | tf_op jit(solution)/shard_map/psum | solution.py:75
  109.9 0.7 copy-start.1
  114.4 90.6 %all-reduce.8.cloned.1.call-start = ((), (), s32[]{:S(2)}) async-start(), calls=%async_computation.6 | async-start | bytes 524288 | tf_op jit(solution)/shard_map/psum | solution.py:77
  205.0 3.8 %copy-start.3 = (bf16[128,1024]{1,0:T(8,128)(2,1)S(1)}, bf16[128,1024]{1,0:T(8,128)(2,1)}, u32[]{:S(2)}) copy-start(bf16[128,1024]{1,0:T(8,128)(2,1)} %all-reduce.8.cloned.1.call-done) | copy-start | bytes 786436
Sparse Core Ops, SparseCore 0:
  21.0 53.8 reduce-scatter.1
  114.5 53.2 all-reduce.5
Sparse Core Ops, SparseCore 1:
  61.3 47.2 all-reduce.3
  170.0 34.9 all-reduce.7

commit v2 on v1

--- a/solution.py
+++ b/solution.py
@@ -1,8 +1,11 @@
+import functools
 import math
 
 import jax
 import jax.numpy as jnp
 from jax import lax
+from jax.experimental import pallas as pl
+from jax.experimental.pallas import tpu as pltpu
 from jax.sharding import PartitionSpec as P
 
 epsilon = 1e-05
@@ -14,6 +17,101 @@
     return lax.dot_general(
         left, right, (((left_dim,), (right_dim,)), ((), ())), preferred_element_type=f32
     )
+
+
+VMEM = pl.BlockSpec(memory_space=pltpu.VMEM)
+
+
+def meet(axis, size):
+    me = lax.axis_index(axis)
+    barrier = pltpu.get_barrier_semaphore()
+    for step in range(1, size):
+        pl.semaphore_signal(
+            barrier,
+            inc=1,
+            device_id={axis: lax.rem(me + step, size)},
+            device_id_type=pl.DeviceIdType.MESH,
+        )
+    pl.semaphore_wait(barrier, size - 1)
+    return me
+
+
+def send(source, land, send_sem, recv_sem, axis, size, me):
+    copies = []
+    for step in range(1, size):
+        peer = lax.rem(me + step, size)
+        copy = pltpu.make_async_remote_copy(
+            src_ref=source(peer),
+            dst_ref=land.at[step - 1],
+            send_sem=send_sem.at[step - 1],
+            recv_sem=recv_sem.at[step - 1],
+            device_id={axis: peer},
+            device_id_type=pl.DeviceIdType.MESH,
+        )
+        copy.start()
+        copies.append(copy)
+    return copies
+
+
+def exchange_kernel(axis, size, gather, x, out, land, send_sem, recv_sem):
+    me = meet(axis, size)
+    source = (lambda peer: x) if gather else (lambda peer: x.at[peer])
+    copies = send(source, land, send_sem, recv_sem, axis, size, me)
+    out[me] = x[...] if gather else x[me]
+    for step in range(1, size):
+        copies[step - 1].wait()
+        out[lax.rem(me + size - step, size)] = land[step - 1]
+
+
+def sum_kernel(axis, size, scale, x, out, land, share, late, sems):
+    me = meet(axis, size)
+    first = send(lambda peer: x.at[peer], land, sems.at[0], sems.at[1], axis, size, me)
+    total = x[me].astype(f32)
+    for step in range(1, size):
+        first[step - 1].wait()
+        total = total + land[step - 1].astype(f32)
+    share[...] = (total * scale).astype(bf16)
+    second = send(lambda peer: share, late, sems.at[2], sems.at[3], axis, size, me)
+    out[me] = share[...]
+    for step in range(1, size):
+        second[step - 1].wait()
+        out[lax.rem(me + size - step, size)] = late[step - 1]
+
+
+def exchange(x, axis, ident, gather=False):
+    size = lax.axis_size(axis)
+    block = x.shape if gather else x.shape[1:]
+    return pl.pallas_call(
+        functools.partial(exchange_kernel, axis, size, gather),
+        out_shape=jax.ShapeDtypeStruct((size,) + block, x.dtype),
+        in_specs=[VMEM],
+        out_specs=VMEM,
+        scratch_shapes=[
+            pltpu.VMEM((size - 1,) + block, x.dtype),
+            pltpu.SemaphoreType.DMA((size - 1,)),
+            pltpu.SemaphoreType.DMA((size - 1,)),
+        ],
+        compiler_params=pltpu.CompilerParams(collective_id=ident, has_side_effects=True),
+    )(x)
+
+
+def all_sum(terms, axis, ident, scale=1.0):
+    size = lax.axis_size(axis)
+    shares = terms.reshape((size, terms.shape[0] // size) + terms.shape[1:])
+    block = shares.shape[1:]
+    return pl.pallas_call(
+        functools.partial(sum_kernel, axis, size, scale),
+        out_shape=jax.ShapeDtypeStruct(shares.shape, bf16),
+        in_specs=[VMEM],
+        out_specs=VMEM,
+        scratch_shapes=[
+            pltpu.VMEM((size - 1,) + block, bf16),
+            pltpu.VMEM(block, bf16),
+            pltpu.VMEM((size - 1,) + block, bf16),
+            pltpu.SemaphoreType.DMA((4, size - 1)),
+        ],
+        compiler_params=pltpu.CompilerParams(collective_id=ident, has_side_effects=True),
+    )(shares).reshape(terms.shape)
 
 
 def on_device(
@@ -33,7 +131,12 @@
     routed = mean_routed * group_count
     loss_scale = 1.0 / math.sqrt(routed)
 
-    every_route = lax.all_gather(route_index, "batch", axis=0, tiled=True).reshape(-1)
+    every_route = exchange(
+        jnp.pad(route_index, ((0, 7), (0, -route_index.shape[1] % 128)), constant_values=-1),
+        "batch",
+        1,
+        gather=True,
+    )[:, 0, : route_index.shape[1]].reshape(-1)
     live = every_route >= 0
     rank = jnp.cumsum(live.astype(jnp.int32)) - 1
     row_ids = lax.broadcasted_iota(jnp.int32, (routed, live.shape[0]), 0)
@@ -44,10 +147,14 @@
     present = slot_pos >= 0
     safe_slot = jnp.maximum(slot_pos, 0)
     local_rows = jnp.where(present[:, None], jnp.take(student_input, safe_slot, axis=0), 0)
-    routed_input = lax.all_gather(local_rows, "tensor", axis=1, tiled=True).astype(f32)
-    mean_square = jnp.mean(routed_input * routed_input, axis=1, keepdims=True)
-    normed = (routed_input * lax.rsqrt(mean_square + epsilon) * norm_gain[None, :]).astype(bf16)
-    every_normed = lax.all_to_all(normed, "batch", split_axis=1, concat_axis=0, tiled=True)
+    routed_input = exchange(local_rows, "tensor", 2, gather=True).astype(f32)
+    width = routed_input.shape[0] * routed_input.shape[2]
+    mean_square = jnp.sum(routed_input * routed_input, axis=(0, 2), keepdims=True) / width
+    gain = norm_gain.reshape(routed_input.shape[0], 1, -1)
+    normed = (routed_input * lax.rsqrt(mean_square + epsilon) * gain).astype(bf16)
+    normed = jnp.swapaxes(normed, 0, 1).reshape(slot_pos.shape[0], group_count, -1)
+    every_normed = exchange(jnp.swapaxes(normed, 0, 1), "batch", 3)
+    every_normed = every_normed.reshape(live.shape[0], -1)
 
     summed = lax.psum_scatter(
         contract(out_weight, attn_values, 0, 1).astype(bf16),
@@ -58,23 +165,23 @@
     teacher_hidden = (residual_t.astype(f32) + summed).astype(bf16)
 
     rows = contract(select, every_normed, 1, 0).astype(bf16)
-    gate_up = lax.psum(
-        jnp.stack([contract(rows, w_gate, 1, 0), contract(rows, w_up, 1, 0)]).astype(bf16),
-        "batch",
-    ).astype(f32)
-    gate_act, up_act = gate_up[0], gate_up[1]
+    gate_up = jnp.concatenate([contract(rows, w_gate, 1, 0), contract(rows, w_up, 1, 0)])
+    gate_up = all_sum(gate_up.astype(bf16), "batch", 4).astype(f32)
+    gate_act, up_act = gate_up[:routed], gate_up[routed:]
     sigma_gate = jax.nn.sigmoid(gate_act)
     hidden = (gate_act * sigma_gate * up_act).astype(bf16)
     out_part = contract(hidden, w_down, 1, 1)
 
     routed_teacher = jnp.where(present[None, :], jnp.take(teacher_hidden, safe_slot, axis=1), 0)
     target_part = contract(routed_teacher, projector, 0, 0).astype(bf16)
-    every_target = lax.all_to_all(target_part, "batch", split_axis=1, concat_axis=0, tiled=True)
+    target_part = target_part.reshape(slot_pos.shape[0], group_count, -1)
+    every_target = exchange(jnp.swapaxes(target_part, 0, 1), "batch", 5)
+    every_target = every_target.reshape(live.shape[0], -1)
     target_rows = contract(select, every_target, 1, 0)
 
-    misfit = lax.psum((out_part - target_rows).astype(bf16), "tensor").astype(f32)
-    grad_out = (jnp.where(live_row, misfit, 0.0) * loss_scale).astype(bf16)
-    grad_hidden = lax.psum(contract(grad_out, w_down, 1, 0).astype(bf16), "batch").astype(f32)
+    misfit = jnp.where(live_row, out_part - target_rows, 0.0)
+    grad_out = all_sum(misfit.astype(bf16), "tensor", 6, loss_scale)
+    grad_hidden = all_sum(contract(grad_out, w_down, 1, 0).astype(bf16), "batch", 7).astype(f32)
     grad_gate_act = (
         grad_hidden * up_act * sigma_gate * (1.0 + gate_act * (1.0 - sigma_gate))
     ).astype(bf16)

time: 220 us -> 186 us (0.85)
  waiting for transfers between devices: 118 us -> 0.02 us
  Pallas kernels: 0 us -> 112 us
  blocking collectives: 26.4 us -> 0 us
  starting transfers between devices: 9.72 us -> 0.04 us
  other arithmetic: 5.09 us -> 10.6 us
  local copies, waits for them, and re-layouts: 5.87 us -> 9.86 us
    pallas_call x0 -> x7, Pallas kernels: none -> 112 us  [the longest x3 61.4 us: all_sum(): pl.pallas_call(functools.partial(sum_kernel, axis, size, scale), out_shap...]
    psum x3 -> x0, waiting for transfers between devices: 104 us -> none  [the longest x1 51.9 us: on_device(): lax.psum((out_part - target_rows).astype(bf16), 'tensor').astype(f32)]
    all_gather x2 -> x0, blocking collectives: 26.4 us -> none  [the longest x1 15.1 us: on_device(): lax.all_gather(route_index, 'batch', axis=0, tiled=True).reshape(-1)]
    reduce_scatter x1, waiting for transfers between devices: 13.7 us -> 0.01 us  [on_device(): lax.psum_scatter(contract(out_weight, attn_values, 0, 1).astype(bf16), 't...]
    all_to_all x2 -> x0, starting transfers between devices: 9.46 us -> none  [the longest x1 4.88 us: on_device(): lax.all_to_all(normed, 'batch', split_axis=1, concat_axis=0, tiled=True)]
  transfers between devices with their start and end apart: 6 -> 1, of which waited for: 4 -> 0; matrix products, arithmetic and copies ran while one was open for 11% -> 11% of each run, Pallas kernels for 0% -> 34%
where the time goes in v2:
time: 186 us; the launch traced here: 185 us
  Pallas kernels  112 us (60%)
  matrix products  38.3 us (21%)
  between operations  14.3 us (8%)
  other arithmetic  10.6 us (6%)
  local copies, waits for them, and re-layouts  9.86 us (5%)
    pallas_call x3, Pallas kernels, all_sum(): pl.pallas_call(functools.partial(sum_kernel, axis, size, scale), out_shap...  61.4 us
    pallas_call x4, Pallas kernels, exchange(): pl.pallas_call(functools.partial(exchange_kernel, axis, size, gather), ou...  50.1 us
    dot_general x11, matrix products, contract(): lax.dot_general(left, right, (((left_dim,), (right_dim,)), ((), ())), pre...  38.3 us
  transfers between devices with their start and end apart: 1, of which 0 were waited for; matrix products, arithmetic and copies ran while one was open for 11% of the time, Pallas kernels for 34%

profile of v2, /device:TPU:0, one launch (start us, length us, event | category | flops | bytes accessed | tf_op | source)
XLA Modules:
  0.0 184.7 jit_solution(17022893312981474006)
XLA Ops:
  7.2 0.0 reduce-scatter.2.cloned.1.call-start
  7.2 12.8 %convolution_convert_fusion = bf16[8192,256]{1,0:T(8,128)(2,1)} fusion(bf16[1024,8192]{1,0:T(8,128)(2,1)} %param.11, bf16[256,1024]{1,0:T(8,128)(2,1)} %param.10), kind=kOutput, calls=%fused_computation.2 | convolution fusion | flops 4297064448 | bytes 21495808 | tf_op jit(solution)/shard_map/dot_general | solution.py:17
  20.0 0.6 copy-done.10
  20.7 0.6 pad.4.x
  21.3 8.6 %shard_map.129 = s32[4,8,128]{2,1,0:T(8,128)} custom-call(s32[8,128]{1,0:T(8,128)} %pad.4.x), custom_call_target="tpu_custom_call" | custom-call | tf_op jit(solution)/shard_map/pallas_call | solution.py:84
  29.9 0.7 fusion.29
  30.6 0.1 reshape.128
  30.7 0.7 compare_reduce_fusion
  31.4 0.1 ge.39
  31.5 0.3 reduce-window.9
  31.8 0.1 slice.26
  31.9 0.1 slice_reduce_fusion
  32.1 0.1 add_bitcast_fusion
  32.1 0.6 slice.28
  32.8 0.7 gather_fusion
  33.5 0.7 select_select_fusion.x
  34.2 10.6 %shard_map.130 = bf16[8,64,512]{2,1,0:T(8,128)(2,1)} custom-call(bf16[64,512]{1,0:T(8,128)(2,1)} %select_select_fusion.x), custom_call_target="tpu_custom_call" | custom-call | tf_op jit(solution)/shard_map/pallas_call | solution.py:84
  44.8 1.4 fusion.2
  46.2 1.2 fusion.10
  47.5 0.3 copy.15
  47.8 0.3 reshape.121
  48.1 1.0 copy.23
  49.1 15.5 %shard_map.131 = bf16[4,64,1024]{2,1,0:T(8,128)(2,1)} custom-call(bf16[4,64,1024]{2,1,0:T(8,128)(2,1)} %bitcast.83), custom_call_target="tpu_custom_call" | custom-call | tf_op jit(solution)/shard_map/pallas_call | solution.py:84
  64.5 1.4 convolution_convert_fusion.5
  66.0 2.0 %convolution_convert_fusion.3 = bf16[128,1024]{1,0:T(8,128)(2,1)S(1)} fusion(bf16[128,1024]{1,0:T(8,128)(2,1)S(1)} %convolution_convert_fusion.5, bf16[1024,1024]{1,0:T(8,128)(2,1)} %param.17), kind=kOutput, calls=%fused_computation.10 | convolution fusion | flops 268566528 | bytes 2621440 | tf_op jit(solution)/shard_map/dot_general | solution.py:17
  68.0 2.0 %convolution_convert_fusion.4 = bf16[128,1024]{1,0:T(8,128)(2,1)S(1)} fusion(bf16[128,1024]{1,0:T(8,128)(2,1)S(1)} %convolution_convert_fusion.5, bf16[1024,1024]{1,0:T(8,128)(2,1)} %param.16), kind=kOutput, calls=%fused_computation.11 | convolution fusion | flops 268566528 | bytes 2621440 | tf_op jit(solution)/shard_map/dot_general | solution.py:17
  70.1 0.8 pad_maximum_fusion
  70.9 29.0 %shard_map.132 = bf16[4,64,1024]{2,1,0:T(8,128)(2,1)} custom-call(bf16[4,64,1024]{2,1,0:T(8,128)(2,1)} %bitcast.82), custom_call_target="tpu_custom_call" | custom-call | tf_op jit(solution)/shard_map/pallas_call | solution.py:102
  99.9 1.2 iota_compare_fusion.1
  101.1 1.1 fusion.32
  102.2 0.8 copy-done.1
  103.0 0.2 fusion.11
  103.2 0.7 copy-done.3
  103.9 1.6 fusion.33
  105.5 2.0 %add_convert_fusion = bf16[1024,256]{1,0:T(8,128)(2,1)} fusion(bf16[1024,256]{1,0:T(8,128)(2,1)} %reduce-scatter.2.cloned.1.call-done, bf16[1024,256]{1,0:T(8,128)(2,1)S(1)} %copy-done.6), kind=kLoop, calls=%fused_computation.16 | loop fusion | flops 1048576 | bytes 1572864 | tf_op jit(solution)/shard_map/convert_element_type | solution.py:165
  107.5 1.2 copy.17
  108.7 0.7 gather_fusion.1
  109.5 5.1 %convolution_convert_fusion.1 = bf16[64,4096]{1,0:T(8,128)(2,1)S(1)} fusion(bf16[1024,4096]{1,0:T(8,128)(2,1)} %param.13, bf16[64,1024]{1,0:T(8,128)(2,1)S(1)} %gather_fusion.1, pred[64]{0:T(512)(128)(4,1)S(1)} %get-tuple-element.8, pred[64]{0:T(512)(128)(4,1)S(1)} %get-tuple-element.9), kind=kOutput, calls=%fused_computation.3 | convolution fusion | flops 537264128 | bytes 9044096 | tf_op jit(solution)/shard_map/dot_general | solution.py:17
  114.5 0.8 copy.22
  115.4 15.5 %shard_map.133 = bf16[4,64,1024]{2,1,0:T(8,128)(2,1)} custom-call(bf16[4,64,1024]{2,1,0:T(8,128)(2,1)} %bitcast.85), custom_call_target="tpu_custom_call" | custom-call | tf_op jit(solution)/shard_map/pallas_call | solution.py:84
  130.9 2.0 %fusion.1 = bf16[128,1024]{1,0:T(8,128)(2,1)} fusion(f32[128,1024]{1,0:T(8,128)S(1)} %copy-done.4, bf16[256,1024]{1,0:T(8,128)(2,1)} %bitcast.80, pred[128]{0:T(512)(128)(4,1)} %iota_compare_fusion.1, s32[256]{0:T(256)S(1)} %add_bitcast_fusion, pred[256]{0:T(512)(128)(4,1)S(1)} %copy-done.9), kind=kOutput, calls=%fused_computation.8 | convolution fusion | flops 67567616 | bytes 1312128 | tf_op jit(solution)/shard_map/dot_general | solution.py:17
  132.9 13.5 %shard_map.134 = bf16[8,16,1024]{2,1,0:T(8,128)(2,1)} custom-call(bf16[8,16,1024]{2,1,0:T(8,128)(2,1)} %bitcast.86), custom_call_target="tpu_custom_call" | custom-call | tf_op jit(solution)/shard_map/pallas_call | solution.py:102
  146.4 2.1 %convolution_convert_fusion.2 = bf16[128,1024]{1,0:T(8,128)(2,1)} fusion(bf16[128,1024]{1,0:T(8,128)(2,1)} %bitcast.78, bf16[1024,1024]{1,0:T(8,128)(2,1)S(1)} %copy-done), kind=kOutput, calls=%fused_computation.9 | convolution fusion | flops 268566528 | bytes 2621440 | tf_op jit(solution)/shard_map/dot_general | solution.py:17
  148.5 3.8 %fusion.36 = f32[1024,1024]{1,0:T(8,128)} fusion(bf16[128,1024]{1,0:T(8,128)(2,1)} %bitcast.79, bf16[128,1024]{1,0:T(8,128)(2,1)} %copy-done.3), kind=kOutput, calls=%fused_computation.67 | convolution fusion | flops 268435456 | bytes 4718592 | tf_op jit(solution)/shard_map/dot_general | solution.py:17
  152.3 18.9 %shard_map.135 = bf16[4,32,1024]{2,1,0:T(8,128)(2,1)} custom-call(bf16[4,32,1024]{2,1,0:T(8,128)(2,1)} %bitcast.87), custom_call_target="tpu_custom_call" | custom-call | tf_op jit(solution)/shard_map/pallas_call | solution.py:102
  171.2 1.2 fusion.9
  172.4 2.7 %fusion.35 = f32[1024,1024]{1,0:T(8,128)} fusion(bf16[128,1024]{1,0:T(8,128)(2,1)S(1)} %convolution_convert_fusion.5, bf16[128,1024]{1,0:T(8,128)(2,1)S(1)} %get-tuple-element.4), kind=kOutput, calls=%fused_computation.66 | convolution fusion | flops 268435456 | bytes 4718592 | tf_op jit(solution)/shard_map/dot_general | solution.py:17
  175.1 2.7 %fusion.34 = f32[1024,1024]{1,0:T(8,128)} fusion(bf16[128,1024]{1,0:T(8,128)(2,1)S(1)} %convolution_convert_fusion.5, bf16[128,1024]{1,0:T(8,128)(2,1)S(1)} %get-tuple-element.5), kind=kOutput, calls=%fused_computation.65 | convolution fusion | flops 268435456 | bytes 4718592 | tf_op jit(solution)/shard_map/dot_general | solution.py:17
  (27 shorter events, 0.1 us)
Async XLA Ops:
  7.2 96.7 %copy-start = (bf16[1024,1024]{1,0:T(8,128)(2,1)S(1)}, bf16[1024,1024]{1,0:T(8,128)(2,1)}, u32[]{:S(2)}) copy-start(bf16[1024,1024]{1,0:T(8,128)(2,1)} %param.18) | copy-start | bytes 6291460
  7.2 98.3 %reduce-scatter.2.cloned.1.call-start = ((), (), s32[]{:S(2)}) async-start(), calls=%async_computation.1 | async-start | bytes 4718592 | tf_op jit(solution)/shard_map/reduce_scatter | solution.py:159
  20.0 0.7 copy-start.10
  20.0 12.7 %copy-start.7 = (f32[4096]{0:T(1024)S(1)}, f32[4096]{0:T(1024)}, u32[]{:S(2)}) copy-start(f32[4096]{0:T(1024)} %param.15) | copy-start | bytes 49156
  20.0 12.7 %copy-start.5 = (bf16[256,512]{1,0:T(8,128)(2,1)S(1)}, bf16[256,512]{1,0:T(8,128)(2,1)}, u32[]{:S(2)}) copy-start(bf16[256,512]{1,0:T(8,128)(2,1)} %param.14) | copy-start | bytes 786436
  31.5 36.5 %copy-start.8 = (pred[256]{0:T(512)(128)(4,1)}, pred[256]{0:T(512)(128)(4,1)S(1)}, u32[]{:S(2)}) copy-start(pred[256]{0:T(512)(128)(4,1)S(1)} %ge.39) | copy-start | bytes 772
  70.1 35.4 %copy-start.6 = (bf16[1024,256]{1,0:T(8,128)(2,1)S(1)}, bf16[1024,256]{1,0:T(8,128)(2,1)}, u32[]{:S(2)}) copy-start(bf16[1024,256]{1,0:T(8,128)(2,1)} %param.12) | copy-start | bytes 1572868
  102.2 0.8 copy-start.1
  103.2 0.7 copy-start.3
  109.4 21.4 %copy-start.4 = (f32[128,1024]{1,0:T(8,128)S(1)}, f32[128,1024]{1,0:T(8,128)}, u32[]{:S(2)}) copy-start(f32[128,1024]{1,0:T(8,128)} %fusion.33) | copy-start | bytes 1572868
  109.4 21.4 %copy-start.9 = (pred[256]{0:T(512)(128)(4,1)S(1)}, pred[256]{0:T(512)(128)(4,1)}, u32[]{:S(2)}) copy-start(pred[256]{0:T(512)(128)(4,1)} %copy-done.8) | copy-start | bytes 772
  132.9 38.3 %copy-start.2 = (f32[2,64,1024]{2,1,0:T(8,128)S(1)}, f32[2,64,1024]{2,1,0:T(8,128)}, u32[]{:S(2)}) copy-start(f32[2,64,1024]{2,1,0:T(8,128)} %copy-done.1) | copy-start | bytes 1572868
Sparse Core Ops, SparseCore 0:
  20.2 53.8 reduce-scatter.1
